TPU v7x, 32 devices: a whole 2x2x4 slice. The times are simulated.
32 devices in a mesh: mz: 4 (over z), px: 8 (over y, x, core).
Axes of the slice: x: 2, y: 2, z: 4, core: 2. Of those that a mesh axis runs over, the one named last changes fastest.
Arguments:
- spectra: float32 [3072, 12288], P('px', 'mz'), may hold values from 0 to 10
- w_factor: float32 [48, 3072], P(None, ('px', 'mz')), may hold values from 0.05 to 1
- h_factor: float32 [48, 12288], P(None, ('mz', 'px')), may hold values from 0.05 to 1
Outputs:
- w_final: float32 [48, 3072], P(None, ('px', 'mz'))
- h_final: float32 [48, 12288], P(None, ('mz', 'px'))
- misfit: float32 [3072], P(('px', 'mz'))
All inputs are finite; a program needn't handle non-finite values.
Results may differ from a plain program's by a relative error of at most 0.0001.
Values sent between devices are 32-bit elements; how exact they have to be, the bound alone decides.
No kernel may reach another device: no remote copies, remote signals or barrier semaphores. Data moves between devices by JAX's collectives and lax.ppermute only.
A program may use at most 64 MiB of HBM per device.

v0:
```python
import jax
import jax.numpy as jnp
from jax import lax
from jax.sharding import PartitionSpec as P

ITERS = 3


def matmul(left, right):
    return jnp.dot(left, right, preferred_element_type=jnp.float32, precision=lax.Precision.HIGHEST)


def rows_of(w_piece):
    return lax.all_gather(w_piece, "mz", axis=1, tiled=True)


def loading_gram(w_block):
    return lax.psum(matmul(w_block, w_block.T), "px")


def spectral_gram(h_block):
    return lax.psum(matmul(h_block, h_block.T), "mz")


def per_device(spectra, w_factor, h_factor):
    w_piece = w_factor
    h_piece = h_factor
    w_block = rows_of(w_piece)
    h_block = h_piece
    for iteration in range(ITERS):
        numerator = lax.psum_scatter(
            matmul(w_block, spectra), "px", scatter_dimension=1, tiled=True
        )
        gram_w = loading_gram(w_block)
        h_piece = h_piece * numerator / matmul(gram_w, h_piece)
        h_block = lax.all_gather(h_piece, "px", axis=1, tiled=True)
        numerator = lax.psum_scatter(
            matmul(h_block, spectra.T), "mz", scatter_dimension=1, tiled=True
        )
        gram_h = spectral_gram(h_block)
        w_piece = w_piece * numerator / matmul(gram_h, w_piece)
        w_block = rows_of(w_piece)
    difference = spectra - matmul(w_block.T, h_block)
    partial_error = jnp.sum(difference * difference, axis=1)
    misfit = lax.psum_scatter(partial_error, "mz", scatter_dimension=0, tiled=True)
    return (w_piece, h_piece, misfit)


def solution(mesh):
    in_specs = (P("px", "mz"), P(None, ("px", "mz")), P(None, ("mz", "px")))
    out_specs = (P(None, ("px", "mz")), P(None, ("mz", "px")), P(("px", "mz")))
    return jax.shard_map(
        per_device, mesh=mesh, in_specs=in_specs, out_specs=out_specs, check_vma=False
    )
```

profile of v0, /device:TPU:0, one launch (start us, length us, event | category | flops | bytes accessed | tf_op | source)
XLA Modules:
  0.0 318.1 jit_solution(4339543671412896273)
XLA Ops:
  7.2 0.0 copy-start.3
  7.2 0.0 reduce-scatter.13.cloned.1.call-start
  7.2 15.3 %all-gather = f32[4,96,48]{1,2,0:T(8,128)S(1)} all-gather(f32[1,96,48]{1,2,0:T(8,128)} %bitcast.70), channel_id=1, replica_groups=mesh['mz'=4,'px'=8] {'mz'}, dimensions={0}, use_global_device_ids=true | all-gather | bytes 92160 | tf_op jit(solution)/shard_map/all_gather | solution.py:14
  22.5 0.1 reshape.7
  22.7 6.1 %fusion = f32[48,3072]{1,0:T(8,128)} fusion(f32[384,48]{0,1:T(8,128)S(1)} %reshape.7, f32[384,3072]{1,0:T(8,128)} %param.3), kind=kOutput, calls=%fused_computation.10 | convolution fusion | flops 679477248 | bytes 5382144 | tf_op jit(solution)/shard_map/dot_general | solution.py:10
  28.7 0.0 reduce-scatter.13.cloned.1.call-update
  28.8 0.0 reduce-scatter.19.cloned.1.call-start
  28.8 0.2 fusion.1
  29.0 22.5 %psum.42 = f32[48,48]{1,0:T(8,128)S(1)} all-reduce(f32[48,48]{1,0:T(8,128)S(1)} %fusion.1), channel_id=1, replica_groups=mesh['mz'=4,'px'=8] {'px'}, use_global_device_ids=true, to_apply=%region_1.0 | all-reduce | flops 2304 | bytes 18432 | tf_op jit(solution)/shard_map/psum | solution.py:18
  51.5 11.9 %reduce-scatter.13.cloned.1.call-done = f32[48,384]{1,0:T(8,128)} async-done(((f32[48,3072]{1,0:T(8,128)}), f32[48,384]{1,0:T(8,128)}) %reduce-scatter.13.cloned.1.call-update) | async-done | bytes 73744 | tf_op jit(solution)/shard_map/reduce_scatter | solution.py:31
  63.4 0.0 copy-done.3
  63.4 1.1 convolution_divide_fusion.2
  64.5 10.4 %all_gather.22 = f32[48,3072]{1,0:T(8,128)S(1)} all-gather(f32[48,384]{1,0:T(8,128)S(1)} %convolution_divide_fusion.2), channel_id=1, replica_groups=mesh['mz'=4,'px'=8] {'px'}, dimensions={1}, use_global_device_ids=true | all-gather | bytes 663552 | tf_op jit(solution)/shard_map/all_gather | solution.py:36
  74.8 6.3 %convolution_bitcast_fusion.2 = f32[384,48]{1,0:T(8,128)} fusion(f32[48,3072]{1,0:T(8,128)S(1)} %all_gather.22, f32[384,3072]{1,0:T(8,128)} %param.3), kind=kOutput, calls=%fused_computation.3 | convolution fusion | flops 679477248 | bytes 5382144
  81.1 0.0 reduce-scatter.19.cloned.1.call-update
  81.1 0.0 reduce-scatter.15.cloned.1.call-start
  81.2 0.6 fusion.2
  81.8 19.1 %psum.43 = f32[48,48]{1,0:T(8,128)S(1)} all-reduce(f32[48,48]{1,0:T(8,128)S(1)} %fusion.2), channel_id=1, replica_groups=mesh['mz'=4,'px'=8] {'mz'}, use_global_device_ids=true, to_apply=%region_3.0 | all-reduce | flops 2304 | bytes 18432 | tf_op jit(solution)/shard_map/psum | solution.py:22
  100.9 0.1 reduce-scatter.19.cloned.1.call-done
  101.0 0.9 copy.15
  101.9 0.2 convolution_divide_fusion.5
  102.1 13.3 %all-gather.1 = f32[4,96,48]{1,2,0:T(8,128)S(1)} all-gather(f32[1,96,48]{1,2,0:T(8,128)S(1)} %bitcast.69), channel_id=1, replica_groups=mesh['mz'=4,'px'=8] {'mz'}, dimensions={0}, use_global_device_ids=true | all-gather | bytes 92160 | tf_op jit(solution)/shard_map/all_gather | solution.py:14
  115.4 0.1 reshape.9
  115.6 6.1 %fusion.3 = f32[48,3072]{1,0:T(8,128)} fusion(f32[384,48]{0,1:T(8,128)S(1)} %reshape.9, f32[384,3072]{1,0:T(8,128)} %param.3), kind=kOutput, calls=%fused_computation.13 | convolution fusion | flops 679477248 | bytes 5382144 | tf_op jit(solution)/shard_map/dot_general | solution.py:10
  121.6 0.0 reduce-scatter.15.cloned.1.call-update
  121.7 0.0 reduce-scatter.21.cloned.1.call-start
  121.7 0.2 fusion.4
  121.9 22.5 %psum.44 = f32[48,48]{1,0:T(8,128)S(1)} all-reduce(f32[48,48]{1,0:T(8,128)S(1)} %fusion.4), channel_id=1, replica_groups=mesh['mz'=4,'px'=8] {'px'}, use_global_device_ids=true, to_apply=%region_5.0 | all-reduce | flops 2304 | bytes 18432 | tf_op jit(solution)/shard_map/psum | solution.py:18
  144.4 8.9 %reduce-scatter.15.cloned.1.call-done = f32[48,384]{1,0:T(8,128)} async-done(((f32[48,3072]{1,0:T(8,128)}), f32[48,384]{1,0:T(8,128)}) %reduce-scatter.15.cloned.1.call-update) | async-done | bytes 73744 | tf_op jit(solution)/shard_map/reduce_scatter | solution.py:31
  153.3 1.1 convolution_divide_fusion.1
  154.4 10.5 %all_gather.24 = f32[48,3072]{1,0:T(8,128)S(1)} all-gather(f32[48,384]{1,0:T(8,128)S(1)} %convolution_divide_fusion.1), channel_id=1, replica_groups=mesh['mz'=4,'px'=8] {'px'}, dimensions={1}, use_global_device_ids=true | all-gather | bytes 663552 | tf_op jit(solution)/shard_map/all_gather | solution.py:36
  165.0 6.3 %convolution_bitcast_fusion.1 = f32[384,48]{1,0:T(8,128)} fusion(f32[48,3072]{1,0:T(8,128)S(1)} %all_gather.24, f32[384,3072]{1,0:T(8,128)} %param.3), kind=kOutput, calls=%fused_computation.2 | convolution fusion | flops 679477248 | bytes 5382144
  171.3 0.0 reduce-scatter.21.cloned.1.call-update
  171.3 0.0 reduce-scatter.17.cloned.1.call-start
  171.3 0.6 fusion.5
  172.0 19.1 %psum.45 = f32[48,48]{1,0:T(8,128)S(1)} all-reduce(f32[48,48]{1,0:T(8,128)S(1)} %fusion.5), channel_id=1, replica_groups=mesh['mz'=4,'px'=8] {'mz'}, use_global_device_ids=true, to_apply=%region_7.0 | all-reduce | flops 2304 | bytes 18432 | tf_op jit(solution)/shard_map/psum | solution.py:22
  191.0 0.1 reduce-scatter.21.cloned.1.call-done
  191.2 0.9 copy.17
  192.0 0.2 convolution_divide_fusion.4
  192.2 13.3 %all-gather.2 = f32[4,96,48]{1,2,0:T(8,128)S(1)} all-gather(f32[1,96,48]{1,2,0:T(8,128)S(1)} %bitcast.68), channel_id=1, replica_groups=mesh['mz'=4,'px'=8] {'mz'}, dimensions={0}, use_global_device_ids=true | all-gather | bytes 92160 | tf_op jit(solution)/shard_map/all_gather | solution.py:14
  205.6 0.1 reshape.11
  205.7 6.1 %fusion.6 = f32[48,3072]{1,0:T(8,128)} fusion(f32[384,48]{0,1:T(8,128)S(1)} %reshape.11, f32[384,3072]{1,0:T(8,128)} %param.3), kind=kOutput, calls=%fused_computation.16 | convolution fusion | flops 679477248 | bytes 5382144 | tf_op jit(solution)/shard_map/dot_general | solution.py:10
  211.8 0.0 reduce-scatter.17.cloned.1.call-update
  211.8 0.0 reduce-scatter.23.cloned.1.call-start
  211.9 0.6 dynamic-slice
  213.1 0.2 fusion.7
  213.3 22.4 %psum.46 = f32[48,48]{1,0:T(8,128)S(1)} all-reduce(f32[48,48]{1,0:T(8,128)S(1)} %fusion.7), channel_id=1, replica_groups=mesh['mz'=4,'px'=8] {'px'}, use_global_device_ids=true, to_apply=%region_9.0 | all-reduce | flops 2304 | bytes 18432 | tf_op jit(solution)/shard_map/psum | solution.py:18
  235.7 7.9 %reduce-scatter.17.cloned.1.call-done = f32[48,384]{1,0:T(8,128)} async-done(((f32[48,3072]{1,0:T(8,128)}), f32[48,384]{1,0:T(8,128)}) %reduce-scatter.17.cloned.1.call-update) | async-done | bytes 73744 | tf_op jit(solution)/shard_map/reduce_scatter | solution.py:31
  243.5 1.1 convolution_divide_fusion
  244.6 0.0 copy-start.2
  244.7 10.4 %all_gather.26 = f32[48,3072]{1,0:T(8,128)S(1)} all-gather(f32[48,384]{1,0:T(8,128)S(1)} %convolution_divide_fusion), channel_id=1, replica_groups=mesh['mz'=4,'px'=8] {'px'}, dimensions={1}, use_global_device_ids=true | all-gather | bytes 663552 | tf_op jit(solution)/shard_map/all_gather | solution.py:36
  255.0 6.3 %convolution_bitcast_fusion = f32[384,48]{1,0:T(8,128)} fusion(f32[48,3072]{1,0:T(8,128)S(1)} %all_gather.26, f32[384,3072]{1,0:T(8,128)} %param.3), kind=kOutput, calls=%fused_computation.1 | convolution fusion | flops 679477248 | bytes 5382144
  261.3 0.0 reduce-scatter.23.cloned.1.call-update
  261.3 0.6 fusion.8
  261.9 19.1 %psum.47 = f32[48,48]{1,0:T(8,128)S(1)} all-reduce(f32[48,48]{1,0:T(8,128)S(1)} %fusion.8), channel_id=1, replica_groups=mesh['mz'=4,'px'=8] {'mz'}, use_global_device_ids=true, to_apply=%region_11.0 | all-reduce | flops 2304 | bytes 18432 | tf_op jit(solution)/shard_map/psum | solution.py:22
  281.1 0.0 reduce-scatter.23.cloned.1.call-done
  281.1 0.9 copy.19
  282.0 0.2 convolution_divide_fusion.3
  282.1 0.0 copy-start.1
  282.1 13.3 %all-gather.3 = f32[4,96,48]{1,2,0:T(8,128)S(1)} all-gather(f32[1,96,48]{1,2,0:T(8,128)S(1)} %bitcast.71), channel_id=1, replica_groups=mesh['mz'=4,'px'=8] {'mz'}, dimensions={0}, use_global_device_ids=true | all-gather | bytes 92160 | tf_op jit(solution)/shard_map/all_gather | solution.py:14
  295.5 0.1 reshape.13
  295.6 6.0 %multiply_reduce_fusion = f32[384]{0:T(512)S(1)} fusion(f32[384,3072]{1,0:T(8,128)} %param.3, f32[384,48]{0,1:T(8,128)S(1)} %reshape.13, f32[48,3072]{1,0:T(8,128)S(1)} %all_gather.26), kind=kOutput, calls=%fused_computation | convolution fusion | flops 683015808 | bytes 5383680 | tf_op jit(solution)/shard_map/dot_general | solution.py:10
  301.7 8.9 %all-reduce = f32[384]{0:T(512)S(1)} all-reduce(f32[384]{0:T(512)S(1)} %multiply_reduce_fusion), channel_id=8, replica_groups=mesh['mz'=4,'px'=8] {'mz'}, use_global_device_ids=true, to_apply=%region_13.0.clone | all-reduce | flops 384 | bytes 3072
  310.6 0.6 dynamic-slice.1
  (10 shorter events, 0.2 us)
Async XLA Ops:
  7.2 56.2 %copy-start.3 = (f32[48,384]{1,0:T(8,128)S(1)}, f32[48,384]{1,0:T(8,128)}, u32[]{:S(2)}) copy-start(f32[48,384]{1,0:T(8,128)} %param.5) | copy-start | bytes 221188
  7.2 56.2 %reduce-scatter.13.cloned.1.call-start = ((), (), s32[]{:S(2)}) async-start(), calls=%async_computation.6 | async-start | bytes 663552 | tf_op jit(solution)/shard_map/reduce_scatter | solution.py:31
  28.7 73.1 %copy-start = (f32[48,96]{1,0:T(8,128)S(1)}, f32[48,96]{1,0:T(8,128)}, u32[]{:S(2)}) copy-start(f32[48,96]{1,0:T(8,128)} %param.4) | copy-start | bytes 55300
  28.8 72.3 %reduce-scatter.19.cloned.1.call-start = ((), (), s32[]{:S(2)}) async-start(), calls=%async_computation.9 | async-start | bytes 245760
  81.1 72.2 %reduce-scatter.15.cloned.1.call-start = ((), (), s32[]{:S(2)}) async-start(), calls=%async_computation.7 | async-start | bytes 663552 | tf_op jit(solution)/shard_map/reduce_scatter | solution.py:31
  121.7 69.5 %reduce-scatter.21.cloned.1.call-start = ((), (), s32[]{:S(2)}) async-start(), calls=%async_computation.10 | async-start | bytes 245760
  171.3 40.6 %copy-start.4 = (u32[32]{0:T(128)S(1)}, u32[32]{0:T(128)}, u32[]{:S(2)}) copy-start(u32[32]{0:T(128)} %constant.4) | copy-start | bytes 388
  171.3 72.2 %reduce-scatter.17.cloned.1.call-start = ((), (), s32[]{:S(2)}) async-start(), calls=%async_computation.8 | async-start | bytes 663552 | tf_op jit(solution)/shard_map/reduce_scatter | solution.py:31
  211.8 69.3 %reduce-scatter.23.cloned.1.call-start = ((), (), s32[]{:S(2)}) async-start(), calls=%async_computation.11 | async-start | bytes 245760
  244.6 57.0 %copy-start.2 = (f32[48,384]{1,0:T(8,128)}, f32[48,384]{1,0:T(8,128)S(1)}, u32[]{:S(2)}) copy-start(f32[48,384]{1,0:T(8,128)S(1)} %convolution_divide_fusion) | copy-start | bytes 221188
  282.1 29.1 %copy-start.1 = (f32[48,96]{1,0:T(8,128)}, f32[48,96]{1,0:T(8,128)S(1)}, u32[]{:S(2)}) copy-start(f32[48,96]{1,0:T(8,128)S(1)} %convolution_divide_fusion.3) | copy-start | bytes 55300
Sparse Core Ops, SparseCore 0:
  28.9 34.4 reduce-scatter.12
  81.3 19.6 reduce-scatter.18
  121.8 31.5 reduce-scatter.14
  171.4 19.6 reduce-scatter.20
  211.9 31.5 reduce-scatter.16
  261.4 19.5 reduce-scatter.22
where the time goes:
time: 319 us; the launch traced here: 318 us
  blocking collectives  220 us (69%)
  matrix products  49.4 us (15%)
  waiting for transfers between devices  29 us (9%)
  between operations  15 us (5%)
  local copies, waits for them, and re-layouts  4.36 us (1%)
    psum x3, blocking collectives, loading_gram(): return lax.psum(matmul(w_block, w_block.T), 'px')  67.3 us
    psum x3, blocking collectives, spectral_gram(): return lax.psum(matmul(h_block, h_block.T), 'mz')  57.3 us
    all_gather x4, blocking collectives, rows_of(): return lax.all_gather(w_piece, 'mz', axis=1, tiled=True)  55.3 us
    all_gather x3, blocking collectives, per_device(): h_block = lax.all_gather(h_piece, 'px', axis=1, tiled=True)  31.2 us
    dot_general x16, matrix products, matmul(): jnp.dot(left, right, preferred_element_type=jnp.float32, precision=lax.Pr...  30.5 us
    reduce_scatter x3, waiting for transfers between devices, per_device(): lax.psum_scatter(matmul(w_block, spectra), 'px', scatter_dimension=1, til...  28.7 us
    unnamed x3, matrix products  18.9 us
    unnamed x1, blocking collectives  8.95 us
  transfers between devices with their start and end apart: 6, of which 5 were waited for; matrix products, arithmetic and copies ran while one was open for 1% of the time, Pallas kernels for 0%

commit v1 on v0

--- a/solution.py
+++ b/solution.py
@@ -2,6 +2,7 @@
 import jax.numpy as jnp
 from jax import lax
 from jax.sharding import PartitionSpec as P
+from jax.lax import all_to_all, axis_size
 
 ITERS = 3
 
@@ -33,7 +34,9 @@
         )
         gram_w = loading_gram(w_block)
         h_piece = h_piece * numerator / matmul(gram_w, h_piece)
-        h_block = lax.all_gather(h_piece, "px", axis=1, tiled=True)
+        h_block = jnp.concatenate(
+            all_to_all(jnp.stack([h_piece] * axis_size("px")), "px", 0, 0), axis=1
+        )
         numerator = lax.psum_scatter(
             matmul(h_block, spectra.T), "mz", scatter_dimension=1, tiled=True
         )

time: 319 us -> 326 us (1.022)
  blocking collectives: 220 us -> 227 us
    all_to_all x0 -> x3, blocking collectives: none -> 38.8 us  [per_device(): all_to_all(jnp.stack([h_piece] * axis_size('px')), 'px', 0, 0)]
    all_gather x3 -> x0, blocking collectives: 31.2 us -> none  [per_device(): h_block = lax.all_gather(h_piece, 'px', axis=1, tiled=True)]
  transfers between devices with their start and end apart: 6 -> 6, of which waited for: 5 -> 3; matrix products, arithmetic and copies ran while one was open for 1% -> 1% of each run, Pallas kernels for 0% -> 0%
where the time goes in v1:
time: 326 us; the launch traced here: 325 us
  blocking collectives  227 us (70%)
  matrix products  49.4 us (15%)
  waiting for transfers between devices  28.5 us (9%)
  between operations  15 us (5%)
  local copies, waits for them, and re-layouts  4.61 us (1%)
    psum x3, blocking collectives, loading_gram(): return lax.psum(matmul(w_block, w_block.T), 'px')  67.3 us
    psum x3, blocking collectives, spectral_gram(): return lax.psum(matmul(h_block, h_block.T), 'mz')  57.3 us
    all_gather x4, blocking collectives, rows_of(): return lax.all_gather(w_piece, 'mz', axis=1, tiled=True)  55.1 us
    all_to_all x3, blocking collectives, per_device(): all_to_all(jnp.stack([h_piece] * axis_size('px')), 'px', 0, 0)  38.8 us
    dot_general x16, matrix products, matmul(): jnp.dot(left, right, preferred_element_type=jnp.float32, precision=lax.Pr...  30.5 us
    reduce_scatter x3, waiting for transfers between devices, per_device(): lax.psum_scatter(matmul(w_block, spectra), 'px', scatter_dimension=1, til...  28.4 us
    unnamed x3, matrix products  18.9 us
    unnamed x1, blocking collectives  8.37 us
  transfers between devices with their start and end apart: 6, of which 3 were waited for; matrix products, arithmetic and copies ran while one was open for 1% of the time, Pallas kernels for 0%

profile of v1, /device:TPU:0, one launch (start us, length us, event | category | flops | bytes accessed | tf_op | source)
XLA Modules:
  0.0 324.7 jit_solution(12025614497799748229)
XLA Ops:
  7.2 0.0 reduce-scatter.13.cloned.1.call-start
  7.2 15.3 %all-gather = f32[4,96,48]{1,2,0:T(8,128)S(1)} all-gather(f32[1,96,48]{1,2,0:T(8,128)} %bitcast.92), channel_id=1, replica_groups=mesh['mz'=4,'px'=8] {'mz'}, dimensions={0}, use_global_device_ids=true | all-gather | bytes 92160 | tf_op jit(solution)/shard_map/all_gather | solution.py:15
  22.5 0.1 reshape.37
  22.7 6.1 %fusion.3 = f32[48,3072]{1,0:T(8,128)} fusion(f32[384,48]{0,1:T(8,128)S(1)} %reshape.37, f32[384,3072]{1,0:T(8,128)} %param.3), kind=kOutput, calls=%fused_computation.16 | convolution fusion | flops 679477248 | bytes 5382144 | tf_op jit(solution)/shard_map/dot_general | solution.py:11
  28.7 0.0 reduce-scatter.13.cloned.1.call-update
  28.8 0.0 reduce-scatter.19.cloned.1.call-start
  28.8 0.2 fusion.4
  29.0 22.5 %psum.42 = f32[48,48]{1,0:T(8,128)S(1)} all-reduce(f32[48,48]{1,0:T(8,128)S(1)} %fusion.4), channel_id=1, replica_groups=mesh['mz'=4,'px'=8] {'px'}, use_global_device_ids=true, to_apply=%region_1.0 | all-reduce | flops 2304 | bytes 18432 | tf_op jit(solution)/shard_map/psum | solution.py:19
  51.5 11.9 %reduce-scatter.13.cloned.1.call-done = f32[48,384]{1,0:T(8,128)} async-done(((f32[48,3072]{1,0:T(8,128)}), f32[48,384]{1,0:T(8,128)}) %reduce-scatter.13.cloned.1.call-update) | async-done | bytes 73744 | tf_op jit(solution)/shard_map/reduce_scatter | solution.py:32
  63.4 1.1 convolution_divide_fusion.2
  64.5 0.0 copy-start
  64.5 13.0 %all_to_all.15 = f32[8,48,384]{2,1,0:T(8,128)S(1)} all-to-all(f32[8,48,384]{2,1,0:T(8,128)S(1)} %stack.6), channel_id=1, replica_groups=mesh['mz'=4,'px'=8] {'px'}, dimensions={0} | all-to-all | bytes 1179648 | tf_op jit(solution)/shard_map/all_to_all | solution.py:38
  77.5 6.3 %convolution_bitcast_fusion.2 = f32[384,48]{1,0:T(8,128)} fusion(f32[48,3072]{1,0:T(8,128)S(1)} %bitcast.88, f32[384,3072]{1,0:T(8,128)} %param.3), kind=kOutput, calls=%fused_computation.3 | convolution fusion | flops 679477248 | bytes 5382144
  83.8 0.0 reduce-scatter.19.cloned.1.call-update
  83.9 0.0 reduce-scatter.15.cloned.1.call-start
  83.9 0.6 convolution_bitcast_fusion.5
  84.5 19.2 %psum.43 = f32[48,48]{1,0:T(8,128)S(1)} all-reduce(f32[48,48]{1,0:T(8,128)S(1)} %convolution_bitcast_fusion.5), channel_id=1, replica_groups=mesh['mz'=4,'px'=8] {'mz'}, use_global_device_ids=true, to_apply=%region_3.0 | all-reduce | flops 2304 | bytes 18432 | tf_op jit(solution)/shard_map/psum | solution.py:23
  103.7 0.0 reduce-scatter.19.cloned.1.call-done
  103.7 0.9 copy.18
  104.6 0.2 convolution_divide_fusion.5
  104.7 13.3 %all-gather.1 = f32[4,96,48]{1,2,0:T(8,128)S(1)} all-gather(f32[1,96,48]{1,2,0:T(8,128)S(1)} %bitcast.91), channel_id=1, replica_groups=mesh['mz'=4,'px'=8] {'mz'}, dimensions={0}, use_global_device_ids=true | all-gather | bytes 92160 | tf_op jit(solution)/shard_map/all_gather | solution.py:15
  118.1 0.1 reshape.39
  118.2 6.1 %fusion.5 = f32[48,3072]{1,0:T(8,128)} fusion(f32[384,48]{0,1:T(8,128)S(1)} %reshape.39, f32[384,3072]{1,0:T(8,128)} %param.3), kind=kOutput, calls=%fused_computation.18 | convolution fusion | flops 679477248 | bytes 5382144 | tf_op jit(solution)/shard_map/dot_general | solution.py:11
  124.3 0.0 reduce-scatter.15.cloned.1.call-update
  124.3 0.0 reduce-scatter.21.cloned.1.call-start
  124.3 0.2 fusion.6
  124.5 22.4 %psum.44 = f32[48,48]{1,0:T(8,128)S(1)} all-reduce(f32[48,48]{1,0:T(8,128)S(1)} %fusion.6), channel_id=1, replica_groups=mesh['mz'=4,'px'=8] {'px'}, use_global_device_ids=true, to_apply=%region_5.0 | all-reduce | flops 2304 | bytes 18432 | tf_op jit(solution)/shard_map/psum | solution.py:19
  147.0 8.3 %reduce-scatter.15.cloned.1.call-done = f32[48,384]{1,0:T(8,128)} async-done(((f32[48,3072]{1,0:T(8,128)}), f32[48,384]{1,0:T(8,128)}) %reduce-scatter.15.cloned.1.call-update) | async-done | bytes 73744 | tf_op jit(solution)/shard_map/reduce_scatter | solution.py:32
  155.2 1.1 convolution_divide_fusion.1
  156.4 12.9 %all_to_all.16 = f32[8,48,384]{2,1,0:T(8,128)S(1)} all-to-all(f32[8,48,384]{2,1,0:T(8,128)S(1)} %stack.7), channel_id=1, replica_groups=mesh['mz'=4,'px'=8] {'px'}, dimensions={0} | all-to-all | bytes 1179648 | tf_op jit(solution)/shard_map/all_to_all | solution.py:38
  169.4 6.3 %convolution_bitcast_fusion.1 = f32[384,48]{1,0:T(8,128)} fusion(f32[48,3072]{1,0:T(8,128)S(1)} %bitcast.89, f32[384,3072]{1,0:T(8,128)} %param.3), kind=kOutput, calls=%fused_computation.2 | convolution fusion | flops 679477248 | bytes 5382144
  175.7 0.0 reduce-scatter.21.cloned.1.call-update
  175.7 0.0 reduce-scatter.17.cloned.1.call-start
  175.8 0.6 convolution_bitcast_fusion.4
  176.4 19.1 %psum.45 = f32[48,48]{1,0:T(8,128)S(1)} all-reduce(f32[48,48]{1,0:T(8,128)S(1)} %convolution_bitcast_fusion.4), channel_id=1, replica_groups=mesh['mz'=4,'px'=8] {'mz'}, use_global_device_ids=true, to_apply=%region_7.0 | all-reduce | flops 2304 | bytes 18432 | tf_op jit(solution)/shard_map/psum | solution.py:23
  195.5 0.0 reduce-scatter.21.cloned.1.call-done
  195.5 0.9 copy.20
  196.4 0.2 convolution_divide_fusion.4
  196.6 13.3 %all-gather.2 = f32[4,96,48]{1,2,0:T(8,128)S(1)} all-gather(f32[1,96,48]{1,2,0:T(8,128)S(1)} %bitcast.90), channel_id=1, replica_groups=mesh['mz'=4,'px'=8] {'mz'}, dimensions={0}, use_global_device_ids=true | all-gather | bytes 92160 | tf_op jit(solution)/shard_map/all_gather | solution.py:15
  209.9 0.1 reshape.41
  210.0 6.1 %fusion.7 = f32[48,3072]{1,0:T(8,128)} fusion(f32[384,48]{0,1:T(8,128)S(1)} %reshape.41, f32[384,3072]{1,0:T(8,128)} %param.3), kind=kOutput, calls=%fused_computation.20 | convolution fusion | flops 679477248 | bytes 5382144 | tf_op jit(solution)/shard_map/dot_general | solution.py:11
  216.1 0.0 reduce-scatter.17.cloned.1.call-update
  216.1 0.0 copy-start.4
  216.1 0.0 reduce-scatter.23.cloned.1.call-start
  216.2 0.2 fusion.8
  216.4 22.4 %psum.46 = f32[48,48]{1,0:T(8,128)S(1)} all-reduce(f32[48,48]{1,0:T(8,128)S(1)} %fusion.8), channel_id=1, replica_groups=mesh['mz'=4,'px'=8] {'px'}, use_global_device_ids=true, to_apply=%region_9.0 | all-reduce | flops 2304 | bytes 18432 | tf_op jit(solution)/shard_map/psum | solution.py:19
  238.8 8.2 %reduce-scatter.17.cloned.1.call-done = f32[48,384]{1,0:T(8,128)} async-done(((f32[48,3072]{1,0:T(8,128)}), f32[48,384]{1,0:T(8,128)}) %reduce-scatter.17.cloned.1.call-update) | async-done | bytes 73744 | tf_op jit(solution)/shard_map/reduce_scatter | solution.py:32
  247.0 1.1 convolution_divide_fusion
  248.1 0.0 copy-start.2
  248.2 12.9 %all_to_all.17 = f32[8,48,384]{2,1,0:T(8,128)S(1)} all-to-all(f32[8,48,384]{2,1,0:T(8,128)S(1)} %stack.8), channel_id=1, replica_groups=mesh['mz'=4,'px'=8] {'px'}, dimensions={0} | all-to-all | bytes 1179648 | tf_op jit(solution)/shard_map/all_to_all | solution.py:38
  261.2 6.3 %convolution_bitcast_fusion = f32[384,48]{1,0:T(8,128)} fusion(f32[48,3072]{1,0:T(8,128)S(1)} %bitcast.83, f32[384,3072]{1,0:T(8,128)} %param.3), kind=kOutput, calls=%fused_computation.1 | convolution fusion | flops 679477248 | bytes 5382144
  267.5 0.0 reduce-scatter.23.cloned.1.call-update
  267.5 0.6 dynamic-slice
  268.8 0.6 convolution_bitcast_fusion.3
  269.4 19.0 %psum.47 = f32[48,48]{1,0:T(8,128)S(1)} all-reduce(f32[48,48]{1,0:T(8,128)S(1)} %convolution_bitcast_fusion.3), channel_id=1, replica_groups=mesh['mz'=4,'px'=8] {'mz'}, use_global_device_ids=true, to_apply=%region_11.0 | all-reduce | flops 2304 | bytes 18432 | tf_op jit(solution)/shard_map/psum | solution.py:23
  288.4 0.0 reduce-scatter.23.cloned.1.call-done
  288.4 0.9 copy.22
  289.3 0.2 convolution_divide_fusion.3
  289.4 0.0 copy-start.1
  289.4 13.3 %all-gather.3 = f32[4,96,48]{1,2,0:T(8,128)S(1)} all-gather(f32[1,96,48]{1,2,0:T(8,128)S(1)} %bitcast.93), channel_id=1, replica_groups=mesh['mz'=4,'px'=8] {'mz'}, dimensions={0}, use_global_device_ids=true | all-gather | bytes 92160 | tf_op jit(solution)/shard_map/all_gather | solution.py:15
  302.8 0.1 reshape.43
  302.9 6.0 %multiply_reduce_fusion = f32[384]{0:T(512)S(1)} fusion(f32[384,3072]{1,0:T(8,128)} %param.3, f32[384,48]{0,1:T(8,128)S(1)} %reshape.43, f32[48,3072]{1,0:T(8,128)S(1)} %bitcast.84), kind=kOutput, calls=%fused_computation | convolution fusion | flops 683015808 | bytes 5383680 | tf_op jit(solution)/shard_map/dot_general | solution.py:11
  308.9 8.4 %all-reduce = f32[384]{0:T(512)S(1)} all-reduce(f32[384]{0:T(512)S(1)} %multiply_reduce_fusion), channel_id=8, replica_groups=mesh['mz'=4,'px'=8] {'mz'}, use_global_device_ids=true, to_apply=%region_13.0.clone | all-reduce | flops 384 | bytes 3072
  317.3 0.6 dynamic-slice.1
  (16 shorter events, 0.4 us)
Async XLA Ops:
  7.2 56.2 %copy-start.3 = (f32[48,384]{1,0:T(8,128)S(1)}, f32[48,384]{1,0:T(8,128)}, u32[]{:S(2)}) copy-start(f32[48,384]{1,0:T(8,128)} %param.5) | copy-start | bytes 221188
  7.2 56.2 %reduce-scatter.13.cloned.1.call-start = ((), (), s32[]{:S(2)}) async-start(), calls=%async_computation.9 | async-start | bytes 663552 | tf_op jit(solution)/shard_map/reduce_scatter | solution.py:32
  28.8 74.9 %reduce-scatter.19.cloned.1.call-start = ((), (), s32[]{:S(2)}) async-start(), calls=%async_computation.12 | async-start | bytes 245760
  64.5 40.1 %copy-start = (f32[48,96]{1,0:T(8,128)S(1)}, f32[48,96]{1,0:T(8,128)}, u32[]{:S(2)}) copy-start(f32[48,96]{1,0:T(8,128)} %param.4) | copy-start | bytes 55300
  83.9 71.4 %reduce-scatter.15.cloned.1.call-start = ((), (), s32[]{:S(2)}) async-start(), calls=%async_computation.10 | async-start | bytes 663552 | tf_op jit(solution)/shard_map/reduce_scatter | solution.py:32
  124.3 71.2 %reduce-scatter.21.cloned.1.call-start = ((), (), s32[]{:S(2)}) async-start(), calls=%async_computation.13 | async-start | bytes 245760
  175.7 71.3 %reduce-scatter.17.cloned.1.call-start = ((), (), s32[]{:S(2)}) async-start(), calls=%async_computation.11 | async-start | bytes 663552 | tf_op jit(solution)/shard_map/reduce_scatter | solution.py:32
  216.1 51.4 %copy-start.4 = (u32[32]{0:T(128)S(1)}, u32[32]{0:T(128)}, u32[]{:S(2)}) copy-start(u32[32]{0:T(128)} %constant.4) | copy-start | bytes 388
  216.1 72.3 %reduce-scatter.23.cloned.1.call-start = ((), (), s32[]{:S(2)}) async-start(), calls=%async_computation.14 | async-start | bytes 245760
  248.1 41.1 %copy-start.2 = (f32[48,384]{1,0:T(8,128)}, f32[48,384]{1,0:T(8,128)S(1)}, u32[]{:S(2)}) copy-start(f32[48,384]{1,0:T(8,128)S(1)} %convolution_divide_fusion) | copy-start | bytes 221188
  289.4 28.4 %copy-start.1 = (f32[48,96]{1,0:T(8,128)}, f32[48,96]{1,0:T(8,128)S(1)}, u32[]{:S(2)}) copy-start(f32[48,96]{1,0:T(8,128)S(1)} %convolution_divide_fusion.3) | copy-start | bytes 55300
Sparse Core Ops, SparseCore 0:
  28.9 34.4 reduce-scatter.12
  84.0 18.9 reduce-scatter.18
  124.4 30.7 reduce-scatter.14
  175.8 18.9 reduce-scatter.20
  216.2 30.7 reduce-scatter.16
  267.6 18.8 reduce-scatter.22
